TPU v7x, 32 devices: a whole 2x2x4 slice. The times are simulated.
32 devices in a mesh: dp: 16 (over z, y, core), ctx: 2 (over x).
Axes of the slice: x: 2, y: 2, z: 4, core: 2. Of those that a mesh axis runs over, the one named last changes fastest.
Arguments:
- params: float32 [7087104], P(('dp', 'ctx')), as said below
- moment_one: float32 [7087104], P(('dp', 'ctx')), may hold values from -6 to 6
- moment_two: float32 [7087104], P(('dp', 'ctx')), may hold values from 0.2048 to 0.8192
- inputs: float32 [16, 256, 768], P('dp', 'ctx'), may hold values from -6 to 6
- cotangent: float32 [16, 256, 768], P('dp', 'ctx'), may hold values from -6 to 6
- doc_ids: int32 [16, 256], P('dp'), may hold values from 0 to 3, never falling along the last dimension, each value on 1 to 128 neighbouring positions
Outputs:
- output: float32 [16, 256, 768], P('dp', 'ctx')
- d_input: float32 [16, 256, 768], P('dp', 'ctx')
- grads: float32 [7087104], P(('dp', 'ctx'))
- new_params: float32 [7087104], P(('dp', 'ctx'))
- new_moment_one: float32 [7087104], P(('dp', 'ctx'))
- new_moment_two: float32 [7087104], P(('dp', 'ctx'))
Inputs may be any that keep to these rules, and one draw needn't show every extreme that they name: `doc_ids`: within a sequence the numbers never fall; each of the 4 documents holds 1 to 128 tokens, and one holds exactly 128. `params`: gains lie near one and biases are of order 0.3; a matrix's entries may be up to some 16 times its fan-in scale.
All inputs are finite; a program needn't handle non-finite values.
Results may differ from a plain program's by a relative error of at most 0.02.
The roundings to bfloat16 on the way count: a program that leaves them out, or rounds other values in their place, can miss the bound.
Values may be sent and summed in bfloat16 or wider, within the bound.
No kernel may reach another device: no remote copies, remote signals or barrier semaphores. Data moves between devices by JAX's collectives and lax.ppermute only.
A program may use at most 256 MiB of HBM per device.

v0:
```python
import math

import jax
import jax.numpy as jnp
from jax import lax
from jax.sharding import PartitionSpec as P

D = 768
HEAD_DIM = 64
FF = 3072
STEP = 3


beta_one = 0.9
beta_two = 0.999
learn_rate = 0.02
decay_rate = 0.1
adam_eps = 1e-08
norm_eps = 1e-05


def unpack(flat, width, hidden_width):
    layouts = [
        (width,),
        (width,),
        (width, width),
        (width,),
        (width, width),
        (width, width),
        (width,),
        (width, width),
        (width,),
        (width,),
        (width,),
        (width, hidden_width),
        (hidden_width,),
        (hidden_width, width),
        (width,),
    ]
    pieces = []
    offset = 0
    for layout in layouts:
        number = math.prod(layout)
        pieces.append(lax.slice_in_dim(flat, offset, offset + number).reshape(layout))
        offset += number
    return pieces


def widen(values):
    return values.astype(jnp.float32)


def matmul(left, right):
    return jnp.dot(left, right, preferred_element_type=jnp.float32)


def weight_sum(left, right):
    return jnp.einsum("sra,srb->ab", left, right, preferred_element_type=jnp.float32)


def normalize(values):
    centered = values - jnp.mean(values, -1, keepdims=True)
    factor = lax.rsqrt(jnp.mean(centered * centered, -1, keepdims=True) + norm_eps)
    return (centered * factor, factor)


def norm_back(d_normed, normed, factor):
    return factor * (
        d_normed
        - jnp.mean(d_normed, -1, keepdims=True)
        - normed * jnp.mean(d_normed * normed, -1, keepdims=True)
    )


def pair_heads(values):
    count, rows, width = values.shape
    pairs = width // (2 * HEAD_DIM)
    return values.reshape(count, rows, pairs, 2, HEAD_DIM).transpose(2, 0, 3, 1, 4)


def join_heads(values):
    pairs, count, two, rows, size = values.shape
    return values.transpose(1, 3, 0, 2, 4).reshape(count, rows, pairs * two * size)


def score_pair(query, keys, allowed):
    scores = jnp.einsum("sgqd,sgkd->sgqk", query, keys, preferred_element_type=jnp.float32)
    return jnp.where(allowed[:, None], scores, -jnp.inf)


def body(params, moment_one, moment_two, inputs, cotangent, doc_ids):
    whole = lax.all_gather(params.astype(jnp.bfloat16), ("dp", "ctx"), axis=0, tiled=True)
    (
        gain_one,
        shift_one,
        w_query,
        b_query,
        w_key,
        w_value,
        b_value,
        w_out,
        b_out,
        gain_two,
        shift_two,
        w_up,
        b_up,
        w_down,
        b_down,
    ) = unpack(whole, D, FF)
    rows = inputs.shape[1]
    length = doc_ids.shape[1]
    first = lax.axis_index("ctx") * rows
    scale = HEAD_DIM ** (-0.5)
    normed_one, factor_one = normalize(inputs)
    act_one = (normed_one * widen(gain_one) + widen(shift_one)).astype(jnp.bfloat16)
    query = ((matmul(act_one, w_query) + widen(b_query)) * scale).astype(jnp.bfloat16)
    key_rows = matmul(act_one, w_key).astype(jnp.bfloat16)
    value_rows = (matmul(act_one, w_value) + widen(b_value)).astype(jnp.bfloat16)
    key_all, value_all = (
        lax.all_gather(key_rows, "ctx", axis=1, tiled=True),
        lax.all_gather(value_rows, "ctx", axis=1, tiled=True),
    )
    local_pos = first + jnp.arange(rows, dtype=jnp.int32)
    whole_pos = jnp.arange(length, dtype=jnp.int32)
    local_docs = lax.dynamic_slice_in_dim(doc_ids, first, rows, 1)
    allowed = (local_docs[:, :, None] == doc_ids[:, None, :]) & (
        whole_pos[None, None, :] <= local_pos[None, :, None]
    )
    query_pairs = pair_heads(query)
    key_pairs = pair_heads(key_all)
    value_pairs = pair_heads(value_all)

    def forward_pair(items):
        q_pair, k_pair, v_pair = items
        scores = score_pair(q_pair, k_pair, allowed)
        top = jnp.max(scores, -1, keepdims=True)
        total = top + jnp.log(jnp.sum(jnp.exp(scores - top), -1, keepdims=True))
        probs_b = jnp.exp(scores - total).astype(jnp.bfloat16)
        out = jnp.einsum("sgqk,sgkd->sgqd", probs_b, v_pair, preferred_element_type=jnp.float32)
        return (out.astype(jnp.bfloat16), total[..., 0])

    attended_pairs, log_total = lax.map(forward_pair, (query_pairs, key_pairs, value_pairs))
    attended = join_heads(attended_pairs)
    hidden = inputs + matmul(attended, w_out) + widen(b_out)
    normed_two, factor_two = normalize(hidden)
    act_two = (normed_two * widen(gain_two) + widen(shift_two)).astype(jnp.bfloat16)
    pre = matmul(act_two, w_up) + widen(b_up)
    relu_rows = jnp.maximum(pre, 0.0).astype(jnp.bfloat16)
    output = hidden + matmul(relu_rows, w_down) + widen(b_down)
    cot_b = cotangent.astype(jnp.bfloat16)
    g_b_down = jnp.sum(cotangent, (0, 1))
    g_w_down = weight_sum(relu_rows, cot_b)
    d_pre = jnp.where(pre > 0, matmul(cot_b, w_down.T), 0.0)
    d_pre_b = d_pre.astype(jnp.bfloat16)
    g_b_up = jnp.sum(d_pre, (0, 1))
    g_w_up = weight_sum(act_two, d_pre_b)
    d_act_two = matmul(d_pre_b, w_up.T)
    g_gain_two = jnp.sum(d_act_two * normed_two, (0, 1))
    g_shift_two = jnp.sum(d_act_two, (0, 1))
    d_hidden = cotangent + norm_back(d_act_two * widen(gain_two), normed_two, factor_two)
    d_hidden_b = d_hidden.astype(jnp.bfloat16)
    g_b_out = jnp.sum(d_hidden, (0, 1))
    g_w_out = weight_sum(attended, d_hidden_b)
    d_attended = matmul(d_hidden_b, w_out.T).astype(jnp.bfloat16)
    d_att_pairs = pair_heads(d_attended)
    delta = jnp.einsum("gsjqd,gsjqd->gsjq", widen(d_att_pairs), widen(attended_pairs))

    def query_side(items):
        q_pair, k_pair, v_pair, total, dd_pair, dl_pair = items
        probs = jnp.exp(score_pair(q_pair, k_pair, allowed) - total[..., None])
        probs_b = probs.astype(jnp.bfloat16)
        d_probs = jnp.einsum("sgqd,sgkd->sgqk", dd_pair, v_pair, preferred_element_type=jnp.float32)
        d_scores = (probs * (d_probs - dl_pair[..., None])).astype(jnp.bfloat16)
        d_q = jnp.einsum("sgqk,sgkd->sgqd", d_scores, k_pair, preferred_element_type=jnp.float32)
        d_k = jnp.einsum("sgqk,sgqd->sgkd", d_scores, q_pair, preferred_element_type=jnp.float32)
        d_v = jnp.einsum("sgqk,sgqd->sgkd", probs_b, dd_pair, preferred_element_type=jnp.float32)
        return (d_q, d_k, d_v)

    d_q_pairs, d_k_pairs, d_v_pairs = lax.map(
        query_side, (query_pairs, key_pairs, value_pairs, log_total, d_att_pairs, delta)
    )
    d_query_raw = join_heads(d_q_pairs)
    d_key_all = join_heads(d_k_pairs)
    d_value_all = join_heads(d_v_pairs)
    d_key, d_value = (
        lax.psum_scatter(d_key_all, "ctx", scatter_dimension=1, tiled=True),
        lax.psum_scatter(d_value_all, "ctx", scatter_dimension=1, tiled=True),
    )
    d_query_pre = d_query_raw * scale
    g_b_query = jnp.sum(d_query_pre, (0, 1))
    g_b_value = jnp.sum(d_value, (0, 1))
    d_query_b = d_query_pre.astype(jnp.bfloat16)
    d_key_b = d_key.astype(jnp.bfloat16)
    d_value_b = d_value.astype(jnp.bfloat16)
    g_w_query = weight_sum(act_one, d_query_b)
    g_w_key = weight_sum(act_one, d_key_b)
    g_w_value = weight_sum(act_one, d_value_b)
    d_act_one = (
        matmul(d_query_b, w_query.T) + matmul(d_key_b, w_key.T) + matmul(d_value_b, w_value.T)
    )
    g_gain_one = jnp.sum(d_act_one * normed_one, (0, 1))
    g_shift_one = jnp.sum(d_act_one, (0, 1))
    d_input = d_hidden + norm_back(d_act_one * widen(gain_one), normed_one, factor_one)
    gradients = [
        g_gain_one,
        g_shift_one,
        g_w_query,
        g_b_query,
        g_w_key,
        g_w_value,
        g_b_value,
        g_w_out,
        g_b_out,
        g_gain_two,
        g_shift_two,
        g_w_up,
        g_b_up,
        g_w_down,
        g_b_down,
    ]
    local_grad = jnp.concatenate([item.reshape(-1) for item in gradients])
    groups = lax.axis_size("dp")
    members = lax.axis_size("ctx")
    sectioned = local_grad.reshape(groups, members, -1)
    ctx_summed = lax.psum_scatter(sectioned, "ctx", scatter_dimension=1, tiled=True)
    grads = lax.psum_scatter(ctx_summed, "dp", scatter_dimension=0, tiled=True).reshape(-1)
    new_one = beta_one * moment_one + (1.0 - beta_one) * grads
    new_two = beta_two * moment_two + (1.0 - beta_two) * grads * grads
    one_hat = new_one / (1.0 - beta_one**STEP)
    two_hat = new_two / (1.0 - beta_two**STEP)
    new_params = params - learn_rate * (
        one_hat / (jnp.sqrt(two_hat) + adam_eps) + decay_rate * params
    )
    return (output, d_input, grads, new_params, new_one, new_two)


def solution(mesh):
    placed = (
        P(("dp", "ctx")),
        P(("dp", "ctx")),
        P(("dp", "ctx")),
        P("dp", "ctx", None),
        P("dp", "ctx", None),
        P("dp", None),
    )
    return jax.shard_map(
        body,
        mesh=mesh,
        in_specs=placed,
        out_specs=(
            P("dp", "ctx", None),
            P("dp", "ctx", None),
            P(("dp", "ctx")),
            P(("dp", "ctx")),
            P(("dp", "ctx")),
            P(("dp", "ctx")),
        ),
        check_vma=False,
    )
```

profile of v0, /device:TPU:0, one launch (start us, length us, event | category | flops | bytes accessed | tf_op | source)
XLA Modules:
  0.0 1456.2 jit_solution(2494188442473601414)
XLA Ops:
  8.4 5.3 broadcast.220
  13.7 7.6 dynamic-update-slice
  23.7 250.2 %all-reduce.6.cloned.1.call-done = bf16[7087104]{0:T(1024)(128)(2,1)} async-done(((bf16[7087104]{0:T(1024)(128)(2,1)}), bf16[7087104]{0:T(1024)(128)(2,1)}) %all-reduce.6.cloned.1.call-update) | async-done | bytes 14174224
  274.0 4.5 fusion.102
  284.4 7.5 all-gather
  296.8 7.2 all-gather.1
  305.9 21.4 %while.29 = (s32[]{:T(128)}, bf16[6,1,2,128,64]{3,4,2,1,0:T(8,128)(2,1)}, f32[6,1,2,128]{3,2,1,0:T(2,128)}, bf16[6,1,2,128,64]{3,4,2,1,0:T(8,128)(2,1)S(1)}, bf1...) while((s32[]{:T(128)}, ...), condition=%wide.region_5.6_spmd.clone, body=%wide.region_2.5_spmd.clone.sunk | while | flops 17284864 | bytes 1060977 | solution.py:142
  327.3 3.6 slice.106
  330.8 9.2 fusion.101
  340.0 9.3 slice.113
  349.3 8.3 reshape.533
  359.5 3.3 convolution_add_fusion
  374.3 50.6 %while.30 = (s32[]{:T(128)}, f32[6,1,2,128,64]{3,4,2,1,0:T(8,128)}, f32[6,1,2,256,64]{3,4,2,1,0:T(8,128)}, f32[6,1,2,256,64]{3,4,2,1,0:T(8,128)}, bf16[6,1,2,128...) while((s32[]{:T(128)}, f32[6,1,2,128,64]{3,4,2,1,0:T(8,128)}, ...), condition=%wide.region_11.12_spmd.clone, body=%wide.region_10.11_spmd.clone.sunk | while | flops 42434560 | bytes 1914001 | solution.py:179
  439.2 3.2 reshape.546
  445.1 5.7 copy.58
  450.9 5.1 fusion.69
  456.0 10.8 reshape.548
  474.2 3.2 reshape.544
  479.4 3.4 reshape.545
  485.4 20.3 %dynamic-update-slice.3 = f32[7087104]{0:T(1024)} dynamic-update-slice(f32[7087104]{0:T(1024)} %constant_dynamic-update-slice_fusion.9, f32[589824]{0:T(1024)S(1)} %copy-done.15, s32[]{} %constant.106) | dynamic-update-slice | bytes 4718596
  506.9 21.4 %dynamic-update-slice.5 = f32[7087104]{0:T(1024)} dynamic-update-slice(f32[7087104]{0:T(1024)} %constant_dynamic-update-slice_fusion.8, f32[589824]{0:T(1024)} %reshape.544, s32[]{} %constant.108) | dynamic-update-slice | bytes 4718596
  528.3 21.3 %dynamic-update-slice.6 = f32[7087104]{0:T(1024)} dynamic-update-slice(f32[7087104]{0:T(1024)} %dynamic-update-slice.5, f32[589824]{0:T(1024)} %reshape.545, s32[]{} %constant.109) | dynamic-update-slice | bytes 4718596
  556.6 80.5 %dynamic-update-slice.12 = f32[7087104]{0:T(1024)} dynamic-update-slice(f32[7087104]{0:T(1024)} %constant_dynamic-update-slice_fusion.3, f32[2359296]{0:T(1024)} %bitcast.253, s32[]{} %constant.115) | dynamic-update-slice | bytes 18874372
  638.5 80.0 %dynamic-update-slice.14 = f32[7087104]{0:T(1024)} dynamic-update-slice(f32[7087104]{0:T(1024)} %constant_dynamic-update-slice_fusion.2, f32[2359296]{0:T(1024)} %reshape.548, s32[]{} %constant.117) | dynamic-update-slice | bytes 18874372
  719.7 98.7 %while.31 = (u32[]{:T(128)}, f32[7087104]{0:T(1024)}, f32[16,2,221472]{2,1,0:T(2,128)}, u32[]{}, u32[]{}, /*index=5*/u32[]{}, u32[]{}) while((u32[]{:T(128)}, f32[7087104]{0:T(1024)}, f32[16,2,221472]{2,1,0:T(2,128)}, u32[]{}, u32[]{}, /*index=5*/u32[]{}, u32[]{}) %tuple.98), condition=%wide.cond, body=%wide.body.sunk | while | flops 9 | bytes 21264564
  722.9 4.7 reshape.572
  727.6 4.7 constant_dynamic-update-slice_fusion.15
  735.3 4.7 reshape.572
  739.9 4.7 constant_dynamic-update-slice_fusion.15
  747.6 4.7 reshape.572
  752.3 4.7 constant_dynamic-update-slice_fusion.15
  759.9 4.7 reshape.572
  764.6 4.6 constant_dynamic-update-slice_fusion.15
  772.2 4.7 reshape.572
  776.9 4.7 constant_dynamic-update-slice_fusion.15
  784.5 4.7 reshape.572
  789.2 4.6 constant_dynamic-update-slice_fusion.15
  796.8 4.7 reshape.572
  801.5 4.7 constant_dynamic-update-slice_fusion.15
  809.1 4.7 reshape.572
  813.8 4.6 constant_dynamic-update-slice_fusion.15
  818.5 27.5 %copy.50 = f32[16,2,221472]{2,0,1:T(8,128)} copy(f32[16,2,221472]{2,1,0:T(2,128)} %get-tuple-element.232) | data formatting | bytes 56696832 | tf_op jit(solution)/shard_map/reshape | solution.py:224
  846.0 312.9 %reduce-scatter.10.cloned.1.call-done = f32[16,1,221472]{2,0,1:T(8,128)} async-done(((f32[16,2,221472]{2,0,1:T(8,128)}), f32[16,1,221472]{2,0,1:T(8,128)}) %reduce-scatter.10.cloned.1.call-update) | async-done | bytes 14174224
  1158.8 17.7 %copy.51 = f32[16,1,221472]{2,1,0:T(1,128)} copy(f32[16,1,221472]{2,0,1:T(8,128)} %reduce-scatter.10.cloned.1.call-done) | data formatting | bytes 28348416 | tf_op jit(solution)/shard_map/reduce_scatter | solution.py:225
  1178.1 3.9 fusion.53
  1182.9 252.6 %all-reduce.8.cloned.1.call-done = f32[16,1,221472]{2,1,0:T(1,128)} async-done(((f32[16,1,221472]{2,1,0:T(1,128)}), f32[16,1,221472]{2,1,0:T(1,128)}) %all-reduce.8.cloned.1.call-update) | async-done | bytes 14174224
  1435.5 9.9 dynamic-slice_reduce_fusion
  1445.4 4.0 multiply_subtract_fusion
  (263 shorter events, 167.3 us)
Async XLA Ops:
  7.2 266.8 %all-reduce.6.cloned.1.call-start = ((), (), s32[]{:S(2)}) async-start(), calls=%async_computation.5 | async-start | bytes 28348416
  21.3 446.0 %reduce-scatter.6.cloned.1.call-start = ((), (), s32[]{:S(2)}) async-start(), calls=%async_computation.3 | async-start | bytes 1179648 | tf_op jit(solution)/shard_map/reduce_scatter | solution.py:186
  23.5 257.3 %copy-start.42 = (f32[128]{0:T(128)}, f32[128]{0:T(128)S(1)}, u32[]{:S(2)}) copy-start(f32[128]{0:T(128)S(1)} %broadcast_multiply_fusion.5) | copy-start | bytes 1540
  23.7 257.1 %copy-start.44 = (f32[128]{0:T(128)}, f32[128]{0:T(128)S(1)}, u32[]{:S(2)}) copy-start(f32[128]{0:T(128)S(1)} %add_rsqrt_fusion.1) | copy-start | bytes 1540
  281.0 14.7 %copy-start.12 = (bf16[128,768]{1,0:T(8,128)(2,1)}, bf16[128,768]{1,0:T(8,128)(2,1)S(1)}, u32[]{:S(2)}) copy-start(bf16[128,768]{1,0:T(8,128)(2,1)S(1)} %fusion.70) | copy-start | bytes 589828
  284.1 9.0 copy-start.9
  295.7 35.1 %copy-start.7 = (bf16[768,768]{1,0:T(8,128)(2,1)}, bf16[768,768]{1,0:T(8,128)(2,1)S(1)}, u32[]{:S(2)}) copy-start(bf16[768,768]{1,0:T(8,128)(2,1)S(1)} %slice.103) | copy-start | bytes 3538948
  327.3 12.7 copy-start.19
  327.3 12.7 copy-start.26
  349.3 8.3 copy-start.10
  349.3 8.3 copy-start.27
  349.3 8.3 copy-start.35
  357.6 5.3 copy-start
  357.6 5.3 copy-start.24
  358.1 84.4 %copy-start.3 = (f32[1,128,768]{2,1,0:T(8,128)}, f32[1,128,768]{2,1,0:T(8,128)S(1)}, u32[]{:S(2)}) copy-start(f32[1,128,768]{2,1,0:T(8,128)S(1)} %get-tuple-element.320) | copy-start | bytes 1179652
  358.1 10.0 copy-start.32
  358.3 9.8 copy-start.41
  359.5 5.7 slice-start
  362.9 88.0 %copy-start.1 = (f32[128,3072]{1,0:T(8,128)}, f32[128,3072]{1,0:T(8,128)S(1)}, u32[]{:S(2)}) copy-start(f32[128,3072]{1,0:T(8,128)S(1)} %convolution_add_fusion) | copy-start | bytes 4718596
  365.2 4.5 copy-start.11
  425.0 44.3 %reduce-scatter.8.cloned.1.call-start = ((), (), s32[]{:S(2)}) async-start(), calls=%async_computation.4 | async-start | bytes 1179648 | tf_op jit(solution)/shard_map/reduce_scatter | solution.py:187
  429.7 729.2 %reduce-scatter.10.cloned.1.call-start = ((), (), s32[]{:S(2)}) async-start(), calls=%async_computation.7 | async-start | bytes 42541056
  434.9 7.6 copy-start.33
  445.1 5.7 copy-start.25
  456.0 10.8 copy-start.29
  456.0 13.4 copy-start.43
  456.0 13.4 copy-start.45
  466.8 2.6 copy-start.8
  466.8 5.4 copy-start.13
  467.3 4.9 copy-start.28
  471.5 5.9 copy-start.21
  471.5 5.9 copy-start.23
  479.4 6.0 copy-start.15
  479.4 26.2 %copy-start.39 = (f32[768]{0:T(1024)S(1)}, f32[768]{0:T(1024)}, u32[]{:S(2)}) copy-start(f32[768]{0:T(1024)} %reduce_sum.175) | copy-start | bytes 9220
  506.9 44.2 %copy-start.14 = (f32[589824]{0:T(1024)S(1)}, f32[589824]{0:T(1024)}, u32[]{:S(2)}) copy-start(f32[589824]{0:T(1024)} %reshape.546) | copy-start | bytes 7077892
  528.3 24.4 %copy-start.38 = (f32[768]{0:T(1024)S(1)}, f32[768]{0:T(1024)}, u32[]{:S(2)}) copy-start(f32[768]{0:T(1024)} %get-tuple-element.296) | copy-start | bytes 9220
  528.3 25.7 %copy-start.40 = (f32[768]{0:T(1024)S(1)}, f32[768]{0:T(1024)}, u32[]{:S(2)}) copy-start(f32[768]{0:T(1024)} %get-tuple-element.233) | copy-start | bytes 9220
  528.3 27.0 %copy-start.37 = (f32[768]{0:T(1024)S(1)}, f32[768]{0:T(1024)}, u32[]{:S(2)}) copy-start(f32[768]{0:T(1024)} %get-tuple-element.237) | copy-start | bytes 9220
  556.6 80.5 %copy-start.31 = (f32[3072]{0:T(1024)S(1)}, f32[3072]{0:T(1024)}, u32[]{:S(2)}) copy-start(f32[3072]{0:T(1024)} %get-tuple-element.323) | copy-start | bytes 36868
  638.5 80.0 %copy-start.36 = (f32[768]{0:T(1024)S(1)}, f32[768]{0:T(1024)}, u32[]{:S(2)}) copy-start(f32[768]{0:T(1024)} %get-tuple-element.316) | copy-start | bytes 9220
  845.9 589.6 %all-reduce.8.cloned.1.call-start = ((), (), s32[]{:S(2)}) async-start(), calls=%async_computation.6 | async-start | bytes 28360704
  1176.6 5.3 copy-start.48
  1176.7 5.3 copy-start.47
  1176.7 5.3 copy-start.6
  1176.7 5.3 copy-start.18
  1176.7 5.3 copy-start.22
  1176.7 5.3 copy-start.46
  1445.4 4.0 copy-start.20
  (9 other events, 13.1 us)
Sparse Core Ops, SparseCore 0:
  21.4 252.4 all-reduce.5
  425.1 16.0 reduce-scatter.5
  444.0 17.4 reduce-scatter.7
  846.1 312.7 reduce-scatter.9
  1176.8 258.6 all-reduce.7
where the time goes:
time: 1480 us; the launch traced here: 1460 us
  waiting for transfers between devices  816 us (55%)
  local copies, waits for them, and re-layouts  488 us (33%)
  matrix products  91.2 us (6%)
  other arithmetic  31.3 us (2%)
    unnamed x8, waiting for transfers between devices  816 us
    unnamed x146, local copies, waits for them, and re-layouts  356 us
    slice x7, local copies, waits for them, and re-layouts, unpack(): lax.slice_in_dim(flat, offset, offset + number).reshape(layout)  32.7 us
  transfers between devices with their start and end apart: 5, of which 3 were waited for; matrix products, arithmetic and copies ran while one was open for 3% of the time, Pallas kernels for 0%

commit v1 on v0

v1 whole, which is shorter than its diff:
```python
import math

import jax
import jax.numpy as jnp
from jax import lax
from jax.experimental import pallas as pl
from jax.experimental.pallas import tpu as pltpu
from jax.sharding import Mesh
from jax.sharding import PartitionSpec as P

HEAD_DIM = 64
STEP = 3
LANES = 128
TILE = 16
BLOCK = LANES * TILE

beta_one = 0.9
beta_two = 0.999
learn_rate = 0.02
decay_rate = 0.1
adam_eps = 1e-08
norm_eps = 1e-05

SLOTS = 4


def layout_rows(width, hidden):
    shapes = [
        ("gain_one", (1, width)),
        ("shift_one", (1, width)),
        ("w_query", (width, width)),
        ("b_query", (1, width)),
        ("w_key", (width, width)),
        ("w_value", (width, width)),
        ("b_value", (1, width)),
        ("w_out", (width, width)),
        ("b_out", (1, width)),
        ("gain_two", (1, width)),
        ("shift_two", (1, width)),
        ("w_up", (width, hidden)),
        ("b_up", (1, hidden)),
        ("w_down", (hidden, width)),
        ("b_down", (1, width)),
    ]
    places = {}
    row = 0
    for name, shape in shapes:
        places[name] = (row, shape)
        row += math.prod(shape) // LANES
    return places


class Windows:
    def __init__(self, total, owners):
        self.owners = owners
        self.size = total // owners
        self.starts = [i * self.size // BLOCK * TILE for i in range(owners)]
        self.rows = max(
            -(-((i + 1) * self.size - s * LANES) // BLOCK) * TILE
            for i, s in enumerate(self.starts)
        )
        self.flat_rows = max(-(-total // BLOCK) * TILE, self.starts[-1] + self.rows)

    def start(self, i):
        return i * self.size // BLOCK * TILE


def widen(values):
    return values.astype(jnp.float32)


def matmul(left, right):
    return jnp.dot(left, right, preferred_element_type=jnp.float32)


def normalize(values):
    centered = values - jnp.mean(values, -1, keepdims=True)
    factor = lax.rsqrt(jnp.mean(centered * centered, -1, keepdims=True) + norm_eps)
    return (centered * factor, factor)


def norm_back(d_normed, normed, factor):
    return factor * (
        d_normed
        - jnp.mean(d_normed, -1, keepdims=True)
        - normed * jnp.mean(d_normed * normed, -1, keepdims=True)
    )


def pair_heads(values):
    count, rows, width = values.shape
    pairs = width // (2 * HEAD_DIM)
    return values.reshape(count, rows, pairs, 2, HEAD_DIM).transpose(2, 0, 3, 1, 4)


def join_heads(values):
    pairs, count, two, rows, size = values.shape
    return values.transpose(1, 3, 0, 2, 4).reshape(count, rows, pairs * two * size)


def score_pair(query, keys, allowed):
    scores = jnp.einsum("sgqd,sgkd->sgqk", query, keys, preferred_element_type=jnp.float32)
    return jnp.where(allowed[:, None], scores, -jnp.inf)


MATRICES = ("w_query", "w_key", "w_value", "w_out", "w_up", "w_down")
VECTORS = (
    "gain_one",
    "shift_one",
    "b_query",
    "b_value",
    "b_out",
    "gain_two",
    "shift_two",
    "b_up",
    "b_down",
)


def read_weights(gathered, places, win):
    def kernel(src, *refs):
        outs = refs[: len(MATRICES) + len(VECTORS)]
        flat, ring, sems = refs[len(outs) :]

        def fetch(i, slot):
            return pltpu.make_async_copy(src.at[i], ring.at[slot], sems.at[slot])

        for i in range(min(SLOTS, win.owners)):
            fetch(i, i).start()

        def place(i, carry):
            slot = lax.rem(i, SLOTS)
            fetch(i, slot).wait()
            base = pl.multiple_of(win.start(i), TILE)
            head = widen(ring[slot, :TILE, :])
            before = flat[pl.ds(base, TILE), :]
            flat[pl.ds(base, TILE), :] = jnp.where(i > 0, before, 0.0) + head
            flat[pl.ds(base + TILE, win.rows - TILE), :] = widen(ring[slot, TILE:, :])

            @pl.when(i + SLOTS < win.owners)
            def _():
                fetch(i + SLOTS, slot).start()

            return carry

        lax.fori_loop(0, win.owners, place, 0)
        for name, out in zip(MATRICES + VECTORS, outs):
            row, (depth, width) = places[name]
            wide = width // LANES
            if depth == 1:
                for c in range(wide):
                    out[:, c * LANES : (c + 1) * LANES] = flat[row + c : row + c + 1, :]
                continue
            step = 256

            def move(k, carry):
                for c in range(wide):
                    part = flat[pl.ds(row + k * (step * wide) + c, step, stride=wide), :]
                    out[pl.ds(pl.multiple_of(k * step, step), step), c * LANES : (c + 1) * LANES] = (
                        part.astype(jnp.bfloat16)
                    )
                return carry

            lax.fori_loop(0, depth // step, move, 0)

    shapes = [jax.ShapeDtypeStruct(places[n][1], jnp.bfloat16) for n in MATRICES]
    shapes += [jax.ShapeDtypeStruct(places[n][1], jnp.float32) for n in VECTORS]
    values = pl.pallas_call(
        kernel,
        out_shape=shapes,
        in_specs=[pl.BlockSpec(memory_space=pl.ANY)],
        out_specs=[pl.BlockSpec(memory_space=pltpu.VMEM)] * len(shapes),
        scratch_shapes=[
            pltpu.VMEM((win.flat_rows, LANES), jnp.float32),
            pltpu.VMEM((SLOTS, win.rows, LANES), jnp.bfloat16),
            pltpu.SemaphoreType.DMA((SLOTS,)),
        ],
        name="read_weights",
    )(gathered)
    return dict(zip(MATRICES + VECTORS, values))


def write_grads(pairs, vectors, places, win):
    names = list(pairs)
    operands = [item for name in names for item in pairs[name]]
    vec_names = list(vectors)
    total = sum(math.prod(shape) // LANES for _, shape in places.values())

    def kernel(*refs):
        mats = refs[: len(operands)]
        vecs = refs[len(operands) : len(operands) + len(vec_names)]
        out, flat, ring, sems = refs[len(operands) + len(vec_names) :]
        for name, vec in zip(vec_names, vecs):
            row, (_, width) = places[name]
            for c in range(width // LANES):
                flat[row + c : row + c + 1, :] = vec[:, c * LANES : (c + 1) * LANES]
        if win.flat_rows > total:
            flat[total:, :] = jnp.zeros((win.flat_rows - total, LANES), jnp.float32)
        for n, name in enumerate(names):
            left, right = mats[2 * n], mats[2 * n + 1]
            row, (depth, width) = places[name]
            wide = width // LANES
            step = 256

            for k in range(depth // step):
                piece = lax.dot_general(
                    left[:, k * step : (k + 1) * step],
                    right[...],
                    (((0,), (0,)), ((), ())),
                    preferred_element_type=jnp.float32,
                )
                for c in range(wide):
                    flat[pl.ds(row + k * (step * wide) + c, step, stride=wide), :] = piece[
                        :, c * LANES : (c + 1) * LANES
                    ]

        def send(i, slot):
            return pltpu.make_async_copy(ring.at[slot], out.at[i], sems.at[slot])

        def pack(i, carry):
            slot = lax.rem(i, SLOTS)

            @pl.when(i >= SLOTS)
            def _():
                send(i - SLOTS, slot).wait()

            base = pl.multiple_of(win.start(i), TILE)
            ring[slot] = flat[pl.ds(base, win.rows), :].astype(jnp.bfloat16)
            send(i, slot).start()
            return carry

        lax.fori_loop(0, win.owners, pack, 0)
        for i in range(max(0, win.owners - SLOTS), win.owners):
            send(i, i % SLOTS).wait()

    return pl.pallas_call(
        kernel,
        out_shape=jax.ShapeDtypeStruct((win.owners, win.rows, LANES), jnp.bfloat16),
        in_specs=[pl.BlockSpec(memory_space=pltpu.VMEM)] * (len(operands) + len(vec_names)),
        out_specs=pl.BlockSpec(memory_space=pl.ANY),
        scratch_shapes=[
            pltpu.VMEM((win.flat_rows, LANES), jnp.float32),
            pltpu.VMEM((SLOTS, win.rows, LANES), jnp.bfloat16),
            pltpu.SemaphoreType.DMA((SLOTS,)),
        ],
        name="write_grads",
    )(*operands, *[vectors[n] for n in vec_names])


def make_body(groups, members):
    owners = groups * members
    both = ("far", "core", "ctx")

    def body(params, moment_one, moment_two, inputs, cotangent, doc_ids):
        width = inputs.shape[2]
        total = params.shape[0] * owners
        hidden_width = (total - 4 * width * width - 8 * width) // (2 * width + 1)
        places = layout_rows(width, hidden_width)
        win = Windows(total, owners)
        me = lax.axis_index(both)
        offset = me * win.size - me * win.size // BLOCK * BLOCK
        window = lax.dynamic_update_slice(
            jnp.zeros((win.rows * LANES,), jnp.bfloat16), params.astype(jnp.bfloat16), (offset,)
        ).reshape(win.rows, LANES)
        gathered = lax.all_gather(window, both, axis=0)
        w = read_weights(gathered, places, win)

        rows = inputs.shape[1]
        length = doc_ids.shape[1]
        first = lax.axis_index("ctx") * rows
        scale = HEAD_DIM ** (-0.5)
        normed_one, factor_one = normalize(inputs)
        act_one = (normed_one * w["gain_one"] + w["shift_one"]).astype(jnp.bfloat16)
        query = ((matmul(act_one, w["w_query"]) + w["b_query"]) * scale).astype(jnp.bfloat16)
        key_rows = matmul(act_one, w["w_key"]).astype(jnp.bfloat16)
        value_rows = (matmul(act_one, w["w_value"]) + w["b_value"]).astype(jnp.bfloat16)
        key_all, value_all = (
            lax.all_gather(key_rows, "ctx", axis=1, tiled=True),
            lax.all_gather(value_rows, "ctx", axis=1, tiled=True),
        )
        local_pos = first + jnp.arange(rows, dtype=jnp.int32)
        whole_pos = jnp.arange(length, dtype=jnp.int32)
        local_docs = lax.dynamic_slice_in_dim(doc_ids, first, rows, 1)
        allowed = (local_docs[:, :, None] == doc_ids[:, None, :]) & (
            whole_pos[None, None, :] <= local_pos[None, :, None]
        )
        query_pairs = pair_heads(query)
        key_pairs = pair_heads(key_all)
        value_pairs = pair_heads(value_all)

        def forward_pair(items):
            q_pair, k_pair, v_pair = items
            scores = score_pair(q_pair, k_pair, allowed)
            top = jnp.max(scores, -1, keepdims=True)
            sums = top + jnp.log(jnp.sum(jnp.exp(scores - top), -1, keepdims=True))
            probs_b = jnp.exp(scores - sums).astype(jnp.bfloat16)
            out = jnp.einsum("sgqk,sgkd->sgqd", probs_b, v_pair, preferred_element_type=jnp.float32)
            return (out.astype(jnp.bfloat16), sums[..., 0])

        attended_pairs, log_total = lax.map(forward_pair, (query_pairs, key_pairs, value_pairs))
        attended = join_heads(attended_pairs)
        hidden = inputs + matmul(attended, w["w_out"]) + w["b_out"]
        normed_two, factor_two = normalize(hidden)
        act_two = (normed_two * w["gain_two"] + w["shift_two"]).astype(jnp.bfloat16)
        pre = matmul(act_two, w["w_up"]) + w["b_up"]
        relu_rows = jnp.maximum(pre, 0.0).astype(jnp.bfloat16)
        output = hidden + matmul(relu_rows, w["w_down"]) + w["b_down"]
        cot_b = cotangent.astype(jnp.bfloat16)
        g_b_down = jnp.sum(cotangent, (0, 1))
        d_pre = jnp.where(pre > 0, matmul(cot_b, w["w_down"].T), 0.0)
        d_pre_b = d_pre.astype(jnp.bfloat16)
        g_b_up = jnp.sum(d_pre, (0, 1))
        d_act_two = matmul(d_pre_b, w["w_up"].T)
        g_gain_two = jnp.sum(d_act_two * normed_two, (0, 1))
        g_shift_two = jnp.sum(d_act_two, (0, 1))
        d_hidden = cotangent + norm_back(d_act_two * w["gain_two"], normed_two, factor_two)
        d_hidden_b = d_hidden.astype(jnp.bfloat16)
        g_b_out = jnp.sum(d_hidden, (0, 1))
        d_attended = matmul(d_hidden_b, w["w_out"].T).astype(jnp.bfloat16)
        d_att_pairs = pair_heads(d_attended)
        delta = jnp.einsum("gsjqd,gsjqd->gsjq", widen(d_att_pairs), widen(attended_pairs))

        def query_side(items):
            q_pair, k_pair, v_pair, sums, dd_pair, dl_pair = items
            probs = jnp.exp(score_pair(q_pair, k_pair, allowed) - sums[..., None])
            probs_b = probs.astype(jnp.bfloat16)
            d_probs = jnp.einsum(
                "sgqd,sgkd->sgqk", dd_pair, v_pair, preferred_element_type=jnp.float32
            )
            d_scores = (probs * (d_probs - dl_pair[..., None])).astype(jnp.bfloat16)
            d_q = jnp.einsum("sgqk,sgkd->sgqd", d_scores, k_pair, preferred_element_type=jnp.float32)
            d_k = jnp.einsum("sgqk,sgqd->sgkd", d_scores, q_pair, preferred_element_type=jnp.float32)
            d_v = jnp.einsum("sgqk,sgqd->sgkd", probs_b, dd_pair, preferred_element_type=jnp.float32)
            return (d_q, d_k, d_v)

        d_q_pairs, d_k_pairs, d_v_pairs = lax.map(
            query_side, (query_pairs, key_pairs, value_pairs, log_total, d_att_pairs, delta)
        )
        d_query_raw = join_heads(d_q_pairs)
        d_key_all = join_heads(d_k_pairs)
        d_value_all = join_heads(d_v_pairs)
        d_key, d_value = (
            lax.psum_scatter(d_key_all, "ctx", scatter_dimension=1, tiled=True),
            lax.psum_scatter(d_value_all, "ctx", scatter_dimension=1, tiled=True),
        )
        d_query_pre = d_query_raw * scale
        g_b_query = jnp.sum(d_query_pre, (0, 1))
        g_b_value = jnp.sum(d_value, (0, 1))
        d_query_b = d_query_pre.astype(jnp.bfloat16)
        d_key_b = d_key.astype(jnp.bfloat16)
        d_value_b = d_value.astype(jnp.bfloat16)
        d_act_one = (
            matmul(d_query_b, w["w_query"].T)
            + matmul(d_key_b, w["w_key"].T)
            + matmul(d_value_b, w["w_value"].T)
        )
        g_gain_one = jnp.sum(d_act_one * normed_one, (0, 1))
        g_shift_one = jnp.sum(d_act_one, (0, 1))
        d_input = d_hidden + norm_back(d_act_one * w["gain_one"], normed_one, factor_one)
        pairs = {
            "w_query": (act_one[0], d_query_b[0]),
            "w_key": (act_one[0], d_key_b[0]),
            "w_value": (act_one[0], d_value_b[0]),
            "w_out": (attended[0], d_hidden_b[0]),
            "w_up": (act_two[0], d_pre_b[0]),
            "w_down": (relu_rows[0], cot_b[0]),
        }
        vectors = {
            "gain_one": g_gain_one,
            "shift_one": g_shift_one,
            "b_query": g_b_query,
            "b_value": g_b_value,
            "b_out": g_b_out,
            "gain_two": g_gain_two,
            "shift_two": g_shift_two,
            "b_up": g_b_up,
            "b_down": g_b_down,
        }
        vectors = {name: value[None] for name, value in vectors.items()}
        sections = write_grads(pairs, vectors, places, win)
        core = lax.axis_index("core")
        sections = sections.reshape(groups // 2, 2, members, win.rows, LANES)
        keep = lax.dynamic_index_in_dim(sections, core, 1, keepdims=False)
        give = lax.dynamic_index_in_dim(sections, 1 - core, 1, keepdims=False)
        got = lax.ppermute(give, "core", [(0, 1), (1, 0)])
        half = (widen(keep) + widen(got)).astype(jnp.bfloat16)
        half = half.reshape(owners // 2, win.rows, LANES)
        summed = lax.psum_scatter(half, ("far", "ctx"), scatter_dimension=0, tiled=True)
        grads = lax.dynamic_slice(widen(summed).reshape(-1), (offset,), (win.size,))
        new_one = beta_one * moment_one + (1.0 - beta_one) * grads
        new_two = beta_two * moment_two + (1.0 - beta_two) * grads * grads
        one_hat = new_one / (1.0 - beta_one**STEP)
        two_hat = new_two / (1.0 - beta_two**STEP)
        new_params = params - learn_rate * (
            one_hat / (jnp.sqrt(two_hat) + adam_eps) + decay_rate * params
        )
        return (output, d_input, grads, new_params, new_one, new_two)

    return body


def solution(mesh):
    groups, members = mesh.shape["dp"], mesh.shape["ctx"]
    split = Mesh(mesh.devices.reshape(groups // 2, 2, members), ("far", "core", "ctx"))
    dp = ("far", "core")
    flat = P(("far", "core", "ctx"))
    return jax.shard_map(
        make_body(groups, members),
        mesh=split,
        in_specs=(flat, flat, flat, P(dp, "ctx", None), P(dp, "ctx", None), P(dp, None)),
        out_specs=(P(dp, "ctx", None), P(dp, "ctx", None), flat, flat, flat, flat),
        check_vma=False,
    )
```

time: 1480 us -> 452 us (0.31); the launches traced: 1460 us -> 450 us
  waiting for transfers between devices: 816 us -> 292 us
  local copies, waits for them, and re-layouts: 488 us -> 24.8 us
  matrix products: 91.2 us -> 43.6 us
  Pallas kernels: 0 us -> 32.4 us
    unnamed x8 -> x4, waiting for transfers between devices: 816 us -> 0.07 us
    unnamed x146 -> x54, local copies, waits for them, and re-layouts: 356 us -> 3.51 us
    reduce_scatter x0 -> x1, waiting for transfers between devices: none -> 148 us  [body(): lax.psum_scatter(half, ('far', 'ctx'), scatter_dimension=0, tiled=True)]
    all_gather x0 -> x1, waiting for transfers between devices: none -> 106 us  [body(): gathered = lax.all_gather(window, both, axis=0)]
    reshape x8 -> x2, local copies, waits for them, and re-layouts: 69.6 us -> 3.5 us  [join_heads(): values.transpose(1, 3, 0, 2, 4).reshape(count, rows, pairs * two * size)]
    slice x7 -> x0, local copies, waits for them, and re-layouts: 32.7 us -> none  [unpack(): lax.slice_in_dim(flat, offset, offset + number).reshape(layout)]
    pallas_call x0 -> x2, Pallas kernels: none -> 32.4 us  [the longest x1 18.4 us: read_weights(): pl.pallas_call(kernel, out_shape=shapes, in_specs=[pl.BlockSpec(memory_sp...]
    reduce_scatter x1, waiting for transfers between devices: 0.02 us -> 18.6 us  [body(): lax.psum_scatter(d_key_all, 'ctx', scatter_dimension=1, tiled=True)]
  transfers between devices with their start and end apart: 5 -> 5, of which waited for: 3 -> 5; matrix products, arithmetic and copies ran while one was open for 3% -> 4% of each run, Pallas kernels for 0% -> 0%
where the time goes in v1:
time: 452 us; the launch traced here: 450 us
  waiting for transfers between devices  292 us (65%)
  matrix products  43.6 us (10%)
  Pallas kernels  32.4 us (7%)
  other arithmetic  28.1 us (6%)
  local copies, waits for them, and re-layouts  24.8 us (5%)
  blocking collectives  14.6 us (3%)
  between operations  14.4 us (3%)
    reduce_scatter x1, waiting for transfers between devices, body(): lax.psum_scatter(half, ('far', 'ctx'), scatter_dimension=0, tiled=True)  148 us
    all_gather x1, waiting for transfers between devices, body(): gathered = lax.all_gather(window, both, axis=0)  106 us
    dot_general x12, matrix products, matmul(): return jnp.dot(left, right, preferred_element_type=jnp.float32)  22.7 us
    reduce_scatter x1, waiting for transfers between devices, body(): lax.psum_scatter(d_key_all, 'ctx', scatter_dimension=1, tiled=True)  18.6 us
    pallas_call x1, Pallas kernels, read_weights(): pl.pallas_call(kernel, out_shape=shapes, in_specs=[pl.BlockSpec(memory_sp...  18.4 us
    pallas_call x1, Pallas kernels, write_grads(): pl.pallas_call(kernel, out_shape=jax.ShapeDtypeStruct((win.owners, win.ro...  14 us
    ppermute x1, waiting for transfers between devices, body(): got = lax.ppermute(give, 'core', [(0, 1), (1, 0)])  11.8 us
    convert_element_type x1, other arithmetic, body(): half = (widen(keep) + widen(got)).astype(jnp.bfloat16)  9.83 us
  transfers between devices with their start and end apart: 5, of which 5 were waited for; matrix products, arithmetic and copies ran while one was open for 4% of the time, Pallas kernels for 0%

profile of v1, /device:TPU:0, one launch (start us, length us, event | category | flops | bytes accessed | tf_op | source)
XLA Modules:
  0.0 450.0 jit_solution(11484616489366864791)
XLA Ops:
  7.3 1.3 convert_element_type.93
  8.6 4.1 dynamic_update_slice.22
  14.1 105.9 %all-gather.4.cloned.1.call-done.src = bf16[32,1760,128]{2,1,0:T(8,128)(2,1)} async-done(((bf16[1,1760,128]{2,1,0:T(8,128)(2,1)}), bf16[32,1760,128]{2,1,0:T(8,128)(2,1)}) %all-gather.4.cloned.1.call-update) | async-done | bytes 14417936 | tf_op jit(solution)/shard_map/all_gather | solution.py:265
  120.0 18.4 %read_weights.1 = (bf16[768,768]{1,0:T(8,128)(2,1)}, bf16[768,768]{1,0:T(8,128)(2,1)}, bf16[768,768]{1,0:T(8,128)(2,1)}, bf16[768,768]{1,0:T(8,128)(2,1)}, bf16[...) custom-call(bf16[32,1760,128]{2,1,0:T(8,128)(2,1)} %all-gather.4.clo, ...), custom_call_target="tpu_custom_call" | custom-call | tf_op jit(solution)/shard_map/read_weights/pallas_call | solution.py:168
  143.4 1.7 fusion.55
  145.2 1.7 fusion.56
  146.9 7.7 %all-gather.1 = bf16[256,768]{1,0:T(8,128)(2,1)S(1)} all-gather(bf16[128,768]{1,0:T(8,128)(2,1)S(1)} %fusion.56), channel_id=3, replica_groups=mesh['far'=8,'core'=2,'ctx'=2] {'ctx'}, dimensions={0}, use_global_device_ids=true | all-gather | bytes 589824 | tf_op jit(solution)/shard_map/all_gather | solution.py:279
  155.2 6.9 %all-gather = bf16[256,768]{1,0:T(8,128)(2,1)S(1)} all-gather(bf16[128,768]{1,0:T(8,128)(2,1)S(1)} %convolution_convert_fusion.2), channel_id=2, replica_groups=mesh['far'=8,'core'=2,'ctx'=2] {'ctx'}, dimensions={0}, use_global_device_ids=true | all-gather | bytes 589824 | tf_op jit(solution)/shard_map/all_gather | solution.py:278
  162.2 5.5 %while.28 = (s32[]{:T(128)}, bf16[6,1,2,128,64]{3,4,2,1,0:T(8,128)(2,1)S(1)}, f32[6,1,2,128]{3,2,1,0:T(2,128)S(1)}, bf16[6,1,2,128,64]{3,4,2,1,0:T(8,128)(2,1)S(...) while((s32[]{:T(128)}, ...), condition=%wide.region_5.6_spmd.clone, body=%wide.region_2.5_spmd.clone.sunk | while | flops 17284864 | bytes 1060977 | solution.py:300
  168.4 1.8 fusion.81
  170.6 4.3 maximum_convert_fusion
  175.0 2.3 fusion.78
  177.3 1.8 fusion.58
  179.5 0.9 copy-done.6
  181.2 18.3 %while.29 = (s32[]{:T(128)}, f32[6,1,2,128,64]{3,4,2,1,0:T(8,128)}, f32[6,1,2,256,64]{3,4,2,1,0:T(8,128)}, f32[6,1,2,256,64]{3,4,2,1,0:T(8,128)}, bf16[6,1,2,128...) while((s32[]{:T(128)}, f32[6,1,2,128,64]{3,4,2,1,0:T(8,128)}, ...), condition=%wide.region_11.12_spmd.clone, body=%wide.region_10.11_spmd.clone.sunk | while | flops 42434560 | bytes 1914001 | solution.py:336
  181.8 0.8 fusion.148
  182.6 0.8 fusion.150
  183.4 0.8 fusion.149
  184.8 0.8 fusion.148
  185.6 0.8 fusion.150
  186.4 0.8 fusion.149
  187.9 0.8 fusion.148
  188.7 0.8 fusion.150
  190.9 0.8 fusion.148
  191.7 0.8 fusion.150
  193.9 0.8 fusion.148
  194.8 0.8 fusion.150
  197.0 0.8 fusion.148
  197.8 0.8 fusion.150
  199.4 2.4 copy.55
  201.9 1.1 copy.53
  203.9 0.8 copy.57.refs_6_
  206.5 1.2 fusion.67
  208.4 0.8 copy.56.refs_1_
  209.2 1.9 fusion.82
  211.1 6.8 %reduce-scatter.6.cloned.1.call-done = f32[1,128,768]{2,1,0:T(8,128)} async-done(((f32[1,256,768]{2,1,0:T(8,128)}), f32[1,128,768]{2,1,0:T(8,128)}) %reduce-scatter.6.cloned.1.call-update) | async-done | bytes 393232 | tf_op jit(solution)/shard_map/reduce_scatter | solution.py:344
  217.9 1.2 fusion.80
  219.7 18.6 %reduce-scatter.4.cloned.1.call-done = f32[1,128,768]{2,1,0:T(8,128)} async-done(((f32[1,256,768]{2,1,0:T(8,128)}), f32[1,128,768]{2,1,0:T(8,128)}) %reduce-scatter.4.cloned.1.call-update) | async-done | bytes 393232 | tf_op jit(solution)/shard_map/reduce_scatter | solution.py:343
  238.2 1.0 convert_bitcast_fusion.1.refs_3_
  239.8 1.9 fusion.59
  243.1 14.0 %write_grads.1 = bf16[32,1760,128]{2,1,0:T(8,128)(2,1)} custom-call(bf16[128,768]{1,0:T(8,128)(2,1)} %copy-done.1, bf16[128,768]{1,0:T(8,128)(2,1)} %copy.56.refs_1_, bf16[128,768]{1,0:T(8,128)(2,1)} %copy-done.1, bf16[128,768]{1,0:T(8,128)(2,1)} %copy-done.10, bf16[128,768]{1,0:T(8,128)(2,1)} %copy-done.1, bf16[128,768]{1,0:T(8,128)(2,1)} %copy-done.13, ...), custom_call_target="tpu_custom_call" | custom-call | tf_op jit(solution)/shard_map/write_grads/pallas_call | solution.py:236
  257.1 6.5 %dynamic-slice_bitcast_fusion = bf16[8,2,1760,128]{3,2,1,0:T(8,128)(2,1)} fusion(bf16[8,2,2,1760,128]{4,3,2,1,0:T(8,128)(2,1)} %bitcast.248, s32[]{:T(128)S(6)} %select_n.38), kind=kLoop, calls=%fused_computation.63 | loop fusion | bytes 14417924 | tf_op jit(solution)/shard_map/jit(dynamic_index_in_dim)/squeeze | solution.py:384
  263.5 11.8 %collective-permute-done = bf16[8,2,1760,128]{3,2,1,0:T(8,128)(2,1)} collective-permute-done((bf16[8,2,1760,128]{3,2,1,0:T(8,128)(2,1)}, bf16[8,2,1760,128]{3,2,1,0:T(8,128)(2,1)}, u32[]{:S(2)}, u32[]{:S(2)}) %collective-permute-start) | collective-permute-done | bytes 7208992 | tf_op jit(solution)/shard_map/ppermute | solution.py:385
  275.3 9.8 %fusion.48 = bf16[8,2,1760,128]{3,2,1,0:T(8,128)(2,1)} fusion(bf16[8,2,1760,128]{3,2,1,0:T(8,128)(2,1)} %collective-permute-done, bf16[8,2,2,1760,128]{4,3,2,1,0:T(8,128)(2,1)} %bitcast.249, s32[]{:T(128)S(6)} %select_n.37), kind=kLoop, calls=%fused_computation.62 | loop fusion | flops 14417920 | bytes 21626884 | tf_op jit(solution)/shard_map/convert_element_type | solution.py:386
  286.3 4.0 fusion.54
  290.3 0.9 fusion.62
  291.2 148.4 %reduce-scatter.8.cloned.1.call-done = bf16[1,1760,128]{2,1,0:T(8,128)(2,1)} async-done(((bf16[16,1760,128]{2,1,0:T(8,128)(2,1)}), bf16[1,1760,128]{2,1,0:T(8,128)(2,1)}) %reduce-scatter.8.cloned.1.call-update) | async-done | bytes 450576 | tf_op jit(solution)/shard_map/reduce_scatter | solution.py:388
  439.6 3.9 multiply_subtract_fusion
  (171 shorter events, 28.3 us)
Async XLA Ops:
  7.2 112.8 %all-gather.4.cloned.1.call-start = ((), (), s32[]{:S(2)}) async-start(), calls=%async_computation.3 | async-start | bytes 14868480 | tf_op jit(solution)/shard_map/all_gather | solution.py:265
  7.2 6.4 %copy-start = (f32[1,128,768]{2,1,0:T(8,128)S(1)}, f32[1,128,768]{2,1,0:T(8,128)}, u32[]{:S(2)}) copy-start(f32[1,128,768]{2,1,0:T(8,128)} %param.13) | copy-start | bytes 1179652
  7.2 6.5 %copy-start.20 = (s32[1,256]{1,0:T(1,128)S(1)}, s32[1,256]{1,0:T(1,128)}, u32[]{:S(2)}) copy-start(s32[1,256]{1,0:T(1,128)} %param.15) | copy-start | bytes 3076
  7.3 6.5 %copy-start.16 = (f32[1,128,768]{2,1,0:T(8,128)S(1)}, f32[1,128,768]{2,1,0:T(8,128)}, u32[]{:S(2)}) copy-start(f32[1,128,768]{2,1,0:T(8,128)} %param.14) | copy-start | bytes 1179652
  12.7 0.8 copy-start.8
  13.5 204.4 %reduce-scatter.6.cloned.1.call-start = ((), (), s32[]{:S(2)}) async-start(), calls=%async_computation.5 | async-start | bytes 1179648 | tf_op jit(solution)/shard_map/reduce_scatter | solution.py:344
  13.8 161.1 %copy-start.11 = (bf16[128,768]{1,0:T(8,128)(2,1)}, bf16[128,768]{1,0:T(8,128)(2,1)S(1)}, u32[]{:S(2)}) copy-start(bf16[128,768]{1,0:T(8,128)(2,1)S(1)} %get-tuple-element.303.refs_11_) | copy-start | bytes 589828
  143.4 11.5 %copy-start.1 = (bf16[128,768]{1,0:T(8,128)(2,1)}, bf16[128,768]{1,0:T(8,128)(2,1)S(1)}, u32[]{:S(2)}) copy-start(bf16[128,768]{1,0:T(8,128)(2,1)S(1)} %fusion.69.refs_0_.refs_2_.refs_4_) | copy-start | bytes 589828
  145.2 9.6 %copy-start.4 = (bf16[768,768]{1,0:T(8,128)(2,1)S(1)}, bf16[768,768]{1,0:T(8,128)(2,1)}, u32[]{:S(2)}) copy-start(bf16[768,768]{1,0:T(8,128)(2,1)} %get-tuple-element.122) | copy-start | bytes 3538948
  162.2 12.7 %slice-start = ((s8[4718592]{0:T(1024)(128)(4,1)}), s8[524288]{0:T(1024)(128)(4,1)S(1)}, s32[]{:S(2)}) async-start(s8[4718592]{0:T(1024)(128)(4,1)} %bitcast.251), calls=%async_computation.7 | async-start | bytes 1048576
  167.7 0.7 copy-start.14
  168.4 2.2 copy-start.21
  170.2 4.7 %slice-start.1 = ((s8[4718592]{0:T(1024)(128)(4,1)}), s8[4194304]{0:T(1024)(128)(4,1)S(1)}, s32[]{:S(2)}) async-start(s8[4718592]{0:T(1024)(128)(4,1)} %bitcast.251), calls=%async_computation.8 | async-start | bytes 8388608
  170.6 4.3 copy-start.12
  170.6 6.6 %slice-start.2 = ((s8[4718592]{0:T(1024)(128)(4,1)}), s8[4194304]{0:T(1024)(128)(4,1)S(1)}, s32[]{:S(2)}) async-start(s8[4718592]{0:T(1024)(128)(4,1)} %bitcast.253), calls=%async_computation.9 | async-start | bytes 8388608
  175.0 2.3 slice-start.3
  177.3 1.8 copy-start.2
  177.3 2.0 copy-start.17
  179.1 1.3 copy-start.6
  179.4 1.6 copy-start.15
  180.3 0.8 copy-start.9
  199.4 2.4 copy-start.19
  201.8 36.4 %reduce-scatter.4.cloned.1.call-start = ((), (), s32[]{:S(2)}) async-start(), calls=%async_computation.4 | async-start | bytes 1179648 | tf_op jit(solution)/shard_map/reduce_scatter | solution.py:343
  203.0 236.5 %reduce-scatter.8.cloned.1.call-start = ((), (), s32[]{:S(2)}) async-start(), calls=%async_computation.6 | async-start | bytes 7659520 | tf_op jit(solution)/shard_map/reduce_scatter | solution.py:388
  209.2 30.1 %copy-start.5 = (bf16[768,768]{1,0:T(8,128)(2,1)S(1)}, bf16[768,768]{1,0:T(8,128)(2,1)}, u32[]{:S(2)}) copy-start(bf16[768,768]{1,0:T(8,128)(2,1)} %get-tuple-element.122) | copy-start | bytes 3538948
  219.0 22.7 %copy-start.13 = (bf16[128,768]{1,0:T(8,128)(2,1)}, bf16[128,768]{1,0:T(8,128)(2,1)S(1)}, u32[]{:S(2)}) copy-start(bf16[128,768]{1,0:T(8,128)(2,1)S(1)} %get-tuple-element.305.refs_5_) | copy-start | bytes 589828
  239.3 2.5 copy-start.10
  263.5 11.8 %collective-permute-start = (bf16[8,2,1760,128]{3,2,1,0:T(8,128)(2,1)}, bf16[8,2,1760,128]{3,2,1,0:T(8,128)(2,1)}, u32[]{:S(2)}, u32[]{:S(2)}) collective-permute-start(bf16[8,2,1760,128]{3,2,1,0:T(8,128)(2,1)} %dynamic-slice_bitcast_fusion), channel_id=1, source_target_pairs={{0,2},{2,0},{1,3},{3,1},{4,6},{6,4},{5,7},{7,5},{8,10},{10,8},{9,1... | collective-permute-start | bytes 21626888 | tf_op jit(solution)/shard_map/ppermute | solution.py:385
  285.2 0.7 copy-start.22
  285.2 1.1 copy-start.3
  286.3 153.3 %copy-start.18 = (f32[221472]{0:T(1024)S(1)}, f32[221472]{0:T(1024)}, u32[]{:S(2)}) copy-start(f32[221472]{0:T(1024)} %param.11) | copy-start | bytes 2657668
  290.3 149.3 %copy-start.7 = (f32[221472]{0:T(1024)S(1)}, f32[221472]{0:T(1024)}, u32[]{:S(2)}) copy-start(f32[221472]{0:T(1024)} %param.10) | copy-start | bytes 2657668
Sparse Core Ops, SparseCore 0:
  13.6 106.2 all-gather.3
  201.9 15.9 reduce-scatter.5
  220.7 17.4 reduce-scatter.3
  285.3 154.2 reduce-scatter.7
